TPU v7x, 128 devices: a whole 4x4x4 slice. The times are simulated.
128 devices in a mesh: chan: 16 (over y, z), win: 8 (over x, core).
Axes of the slice: x: 4, y: 4, z: 4, core: 2. Of those that a mesh axis runs over, the one named last changes fastest.
Arguments:
- spectra: bfloat16 [768, 32, 2, 1024], P('chan', 'win'), may hold values from -120 to 120
- sources: int32 [4], replicated, may hold values from 0 to 767
- bin_rows: int32 [4, 16, 32, 3], P(None, 'chan'), may hold values from -1 to 47, as said below
Outputs:
- stacked: float32 [4, 32, 4096], P(None, 'chan', 'win')
Inputs may be any that keep to these rules, and one draw needn't show every extreme that they name: `bin_rows`: for every step and every index d of chan, the entries name each of that device's 48 local receiver rows exactly once; within a bin the used slots come first and the rest are -1. In each step one bin uses all 3 slots on every device.
All inputs are finite; a program needn't handle non-finite values.
Results may differ from a plain program's by a relative error of at most 0.0099.
Values may be sent and summed in bfloat16 or wider, within the bound.
No kernel may reach another device: no remote copies, remote signals or barrier semaphores. Data moves between devices by JAX's collectives and lax.ppermute only.
A program may use at most 768 MiB of HBM per device.

v0:
```python
import jax
import jax.numpy as jnp
from jax import lax
from jax.sharding import PartitionSpec as P

F = 1024
F0 = 32
NFFT = 8192
LMAX = 2048
HW = 32
NBINS = 32
MOST = 3
LAGS = 4096
epsilon_amp = 1e-06
phase_floor = 0.1


def broadcast(block, axis, source):
    block = jnp.where(lax.axis_index(axis) == source, block, jnp.zeros_like(block))
    return lax.psum(block, axis)


def band_matrix():
    index = jnp.arange(F, dtype=jnp.int32)
    inside = jnp.abs(index[:, None] - index[None, :]) <= HW
    return inside.astype(jnp.float32) / (2 * HW + 1)


def whiten(spectra):
    real_part = spectra[:, :, 0, :].astype(jnp.float32)
    imag_part = spectra[:, :, 1, :].astype(jnp.float32)
    amplitude = jnp.sqrt(real_part * real_part + imag_part * imag_part)
    smooth = jnp.dot(amplitude.reshape(-1, F), band_matrix(), precision=lax.Precision.HIGHEST)
    smooth = smooth.reshape(amplitude.shape) + epsilon_amp
    return jnp.stack([real_part / smooth, imag_part / smooth], axis=2).astype(jnp.bfloat16)


def cross_spectra(white, source):
    white_real = white[..., 0, :].astype(jnp.float32)
    white_imag = white[..., 1, :].astype(jnp.float32)
    source_real = source[..., 0, :].astype(jnp.float32)
    source_imag = source[..., 1, :].astype(jnp.float32)
    cross_real = white_real * source_real + white_imag * source_imag
    cross_imag = white_imag * source_real - white_real * source_imag
    return jnp.concatenate([cross_real, cross_imag], axis=-1).astype(jnp.bfloat16)


def lag_table(first_lag, lag_count):
    frequency = F0 + jnp.arange(F, dtype=jnp.int32)
    lag_index = first_lag + jnp.arange(lag_count, dtype=jnp.int32) - LMAX
    turn_count = jnp.mod(frequency[:, None] * lag_index[None, :], NFFT)
    angle_rad = turn_count.astype(jnp.float32) * (2.0 * jnp.pi / NFFT)
    cosine = jnp.cos(angle_rad)
    sine_part = jnp.sin(angle_rad)
    upper_half = jnp.concatenate([cosine, sine_part], axis=1)
    lower_half = jnp.concatenate([-sine_part, cosine], axis=1)
    return jnp.concatenate([upper_half, lower_half], axis=0).astype(jnp.bfloat16)


def correlate_block(cross_rows, first_lag, lag_count, windows):
    analytic = jnp.dot(
        cross_rows, lag_table(first_lag, lag_count), preferred_element_type=jnp.float32
    )
    analytic = analytic * (1.0 / jnp.sqrt(jnp.float32(F)))
    real_part = analytic[:, :lag_count]
    imag_part = analytic[:, lag_count:]
    magnitude = jnp.maximum(jnp.sqrt(real_part * real_part + imag_part * imag_part), phase_floor)
    terms = jnp.stack([real_part, real_part / magnitude, imag_part / magnitude], axis=1)
    return terms.reshape(-1, windows, 3, lag_count).sum(axis=1)


def weigh_stack(totals, counts, windows):
    traces = jnp.maximum(counts, 1.0) * windows
    linear = totals[..., 0, :]
    power = totals[..., 1, :] * totals[..., 1, :] + totals[..., 2, :] * totals[..., 2, :]
    return linear / jnp.sqrt(traces)[..., None] * power / traces[..., None]


def gather_rows(partial_value, slot_rows, chan_count):
    is_live = slot_rows >= 0
    safe_rows = jnp.maximum(slot_rows, 0)
    picked = jax.vmap(lambda block_rows, chosen: block_rows[chosen])(partial_value, safe_rows)
    picked = picked * is_live[..., None, None].astype(jnp.float32)
    step_count = slot_rows.shape[0]
    slot_count = NBINS * MOST // chan_count
    buffer = picked.reshape(step_count, chan_count, slot_count, 3, partial_value.shape[-1])
    live_mask = is_live.astype(jnp.float32).reshape(step_count, chan_count, slot_count)
    return (buffer, live_mask)


def fold_slots(received, live_mask):
    step_count, chan_count, slot_count = live_mask.shape
    bin_count = slot_count // MOST
    totals = received.reshape(step_count, chan_count, bin_count, MOST, 3, received.shape[-1]).sum(
        axis=(1, 3)
    )
    counts = live_mask.reshape(step_count, chan_count, bin_count, MOST).sum(axis=(1, 3))
    return (totals, counts)


def shards(spectra, sources, bin_rows):
    chan_dev = spectra.shape[0]
    win_dev = spectra.shape[1]
    chan_count = lax.axis_size("chan")
    windows = win_dev * lax.axis_size("win")
    step_count = sources.shape[0]
    white = whiten(spectra)
    owners = sources // chan_dev
    local_rows = sources % chan_dev
    gathered = []
    for step_index in range(step_count):
        own_row = lax.dynamic_index_in_dim(white, local_rows[step_index], 0, keepdims=False)
        gathered.append(broadcast(own_row, "chan", owners[step_index]))
    source = jnp.stack(gathered)
    cross_rows = cross_spectra(white[None], source[:, None]).reshape(-1, 2 * F)
    block_len = min(256, LAGS)
    block_count = LAGS // block_len

    def one_block(block):
        return correlate_block(cross_rows, block * block_len, block_len, win_dev)

    pieces = lax.map(one_block, jnp.arange(block_count, dtype=jnp.int32))
    pieces = pieces.reshape(block_count, step_count, chan_dev, 3, block_len)
    partial_value = jnp.transpose(pieces, (1, 2, 3, 0, 4)).reshape(step_count, chan_dev, 3, LAGS)
    slot_rows = bin_rows[:, 0]
    buffer, live_mask = gather_rows(partial_value, slot_rows, chan_count)
    received, live_got = (
        lax.all_to_all(buffer, "chan", split_axis=1, concat_axis=1, tiled=True),
        lax.all_to_all(live_mask, "chan", split_axis=1, concat_axis=1, tiled=True),
    )
    totals, counts = fold_slots(received, live_got)
    totals = lax.psum_scatter(totals, "win", scatter_dimension=3, tiled=True)
    return weigh_stack(totals, counts, windows)


def solution(mesh):
    in_specs = (P("chan", "win", None, None), P(), P(None, "chan", None, None))
    out_specs = P(None, "chan", "win")
    return jax.shard_map(shards, mesh=mesh, in_specs=in_specs, out_specs=out_specs, check_vma=False)
```

profile of v0, /device:TPU:0, one launch (start us, length us, event | category | flops | bytes accessed | tf_op | source)
XLA Modules:
  0.0 759.1 jit_solution(268665359414033061)
XLA Ops:
  21.3 4.2 fusion.30
  29.7 82.3 %all-reduce.3.cloned.1.call-done = (bf16[1,4,2,1024]{3,0,1,2:T(2,128)(2,1)}, bf16[1,4,2,1024]{3,0,1,2:T(2,128)(2,1)}, bf16[1,4,2,1024]{3,0,1,2:T(2,128)(2,1)}, bf16[1,4,2,1024]{3,0,1,2:T(2,128)(2,1)}) async-done(((bf16[1,4,2,1024]{3,0,1,2:T(2,128)(2,1)}, bf16[1,4,2,1024]{3,0,1,2:T(2,128)(2,1)}, bf16[1,4,2,1024]{3,0,1,2:T(2,128)(2,1)}, bf16[1,4,2,1024]{3,0,1,2:T(2,128)(2,1)}), ...) | async-done | bytes 65552 | tf_op jit(solution)/shard_map/psum | solution.py:20
  123.0 227.3 %while.12 = (s32[]{:T(128)}, f32[16,192,3,256]{3,1,2,0:T(8,128)}, s32[16]{0:T(128)S(1)}, bf16[768,2048]{1,0:T(8,128)(2,1)}, s32[]{:T(128)}, /*index=5*/s32[1]{0:T(128)}) while((s32[]{:T(128)}, f32[16,192,3,256]{3,1,2,0:T(8,128)}, s32[16]{0:T(128)S(1)}, bf16[768,2048]{1,0:T(8,128)(2,1)}, s32[]{:T(128)}, /*index=5*/s32[1]{0:T(128)}) %tuple.55), condition=%wide.region_6.7_spmd, body=%wide.region_4.6_spmd.sunk | while | flops 1626916352 | bytes 25373280 | solution.py:122
  124.3 4.7 fusion.55
  138.5 4.7 fusion.55
  152.6 4.7 fusion.55
  166.9 4.7 fusion.55
  181.0 4.7 fusion.55
  195.2 4.7 fusion.55
  209.4 4.7 fusion.55
  223.5 4.7 fusion.55
  237.7 4.7 fusion.55
  251.9 4.7 fusion.55
  266.1 4.7 fusion.55
  280.2 4.7 fusion.55
  284.9 3.7 multiply_bitcast_fusion.2
  294.4 4.7 fusion.55
  308.6 4.7 fusion.55
  322.7 4.7 fusion.55
  336.9 4.7 fusion.55
  350.4 13.8 %copy.118 = f32[16,4,48,3,256]{4,0,2,3,1:T(8,128)} copy(f32[16,4,48,3,256]{4,2,1,3,0:T(8,128)} %bitcast.98) | data formatting | bytes 18874368 | tf_op jit(solution)/shard_map/reshape | solution.py:123
  364.2 11.3 %reshape.190 = f32[4,48,3,4096]{3,1,2,0:T(8,128)} reshape(f32[4,48,3,16,256]{4,3,1,2,0:T(8,128)} %bitcast.96) | data formatting | bytes 18874368 | tf_op jit(solution)/shard_map/reshape | solution.py:124
  375.5 14.8 %copy.82 = f32[4,48,3,4096]{3,2,1,0:T(4,128)} copy(f32[4,48,3,4096]{3,1,2,0:T(8,128)} %reshape.190) | data formatting | bytes 18874368 | tf_op jit(solution)/shard_map/reshape | solution.py:124
  390.3 31.4 %gather_fusion = f32[384,3,4096]{2,1,0:T(4,128)} fusion(f32[4,48,3,4096]{3,2,1,0:T(4,128)} %copy.82, s32[384]{0:T(512)S(1)} %reshape.200), kind=kCustom, calls=%fused_computation | custom fusion | bytes 37751808 | tf_op jit(solution)/shard_map/vmap()/gather | solution.py:82
  421.7 12.7 %copy_multiply_fusion = f32[4,16,6,3,4096]{4,2,1,0,3:T(8,128)S(1)} fusion(f32[4,16,6,3,4096]{4,3,2,1,0:T(4,128)} %bitcast.95, f32[4,16,6]{2,1,0:T(8,128)S(1)} %reshape.199), kind=kLoop, calls=%fused_computation.30 | loop fusion | flops 4718592 | bytes 37750272 | tf_op jit(solution)/shard_map/mul | solution.py:83
  434.4 17.2 %copy.85 = f32[4,16,6,3,4096]{4,0,3,2,1:T(4,128)} copy(f32[4,16,6,3,4096]{4,2,1,0,3:T(8,128)S(1)} %copy_multiply_fusion) | data formatting | bytes 37748736 | tf_op jit(solution)/shard_map/mul | solution.py:83
  451.7 213.3 %all_to_all.10 = f32[4,16,6,3,4096]{4,0,3,2,1:T(4,128)} all-to-all(f32[4,16,6,3,4096]{4,0,3,2,1:T(4,128)} %copy.85), channel_id=1, replica_groups=mesh['chan'=16,'win'=8] {'chan'}, dimensions={1} | all-to-all | bytes 37748736 | tf_op jit(solution)/shard_map/all_to_all | solution.py:128
  665.0 10.5 %reduce_sum.44 = f32[4,6,3,4096]{3,0,2,1:T(4,128)S(1)} reduce(f32[4,16,6,3,4096]{4,0,3,2,1:T(4,128)} %all_to_all.10, f32[]{:T(128)} %constant.115.clone.1), dimensions={1}, to_apply=%region_7.8 | reduce | flops 4423680 | bytes 20054020 | tf_op jit(solution)/shard_map/reduce_sum | solution.py:94
  675.8 16.9 %copy.91 = f32[4,2,3,4096]{1,0,2,3:T(4,128)} copy(f32[4,2,3,4096]{3,0,2,1:T(4,128)S(1)} %reduce_sum.46) | data formatting | bytes 786432
  692.7 18.1 %reshape.213 = f32[4096,24]{1,0:T(8,128)} reshape(f32[4096,3,4,2]{3,2,1,0:T(4,128)} %bitcast.94) | data formatting | bytes 786432
  710.8 11.1 %all_to_all.11 = f32[4,16,6]{2,0,1:T(4,128)S(1)} all-to-all(f32[4,16,6]{2,0,1:T(4,128)S(1)} %copy.89), channel_id=1, replica_groups=mesh['chan'=16,'win'=8] {'chan'}, dimensions={1} | all-to-all | bytes 3072 | tf_op jit(solution)/shard_map/all_to_all | solution.py:129
  722.1 20.2 %reduce-scatter.4.cloned.1.call-done = f32[512,24]{1,0:T(8,128)} async-done(((f32[4096,24]{1,0:T(8,128)}), f32[512,24]{1,0:T(8,128)}) %reduce-scatter.4.cloned.1.call-update) | async-done | bytes 49168
  (249 shorter events, 166.3 us)
Async XLA Ops:
  6.5 105.5 %all-reduce.3.cloned.1.call-start = ((), (), s32[]{:S(2)}) async-start(), calls=%async_computation.4 | async-start | bytes 262144 | tf_op jit(solution)/shard_map/psum | solution.py:20
  21.3 5.4 copy-start.1
  26.4 716.0 %reduce-scatter.4.cloned.1.call-start = ((), (), s32[]{:S(2)}) async-start(), calls=%async_computation.3 | async-start | bytes 2359296
  117.8 1.9 copy-start
Sparse Core Ops, SparseCore 0:
  26.5 85.4 all-reduce.2
  710.9 31.3 reduce-scatter.3
where the time goes:
time: 766 us; the launch traced here: 759 us
  blocking collectives  224 us (29%)
  local copies, waits for them, and re-layouts  191 us (25%)
  other arithmetic  141 us (18%)
  waiting for transfers between devices  103 us (13%)
  matrix products  63.9 us (8%)
  between operations  23.8 us (3%)
  loops' own time  11.9 us (2%)
    all_to_all x1, blocking collectives, shards(): lax.all_to_all(buffer, 'chan', split_axis=1, concat_axis=1, tiled=True)  213 us
    psum x1, waiting for transfers between devices, broadcast(): return lax.psum(block, axis)  82.3 us
    another operation x17, other arithmetic  78.3 us
    dot_general x16, matrix products, correlate_block(): jnp.dot(cross_rows, lag_table(first_lag, lag_count), preferred_element_ty...  59.6 us
    unnamed x10, local copies, waits for them, and re-layouts  42.2 us
    gather x3, local copies, waits for them, and re-layouts, gather_rows(): block_rows[chosen]  31.7 us
    reduce_sum x16, other arithmetic, correlate_block(): return terms.reshape(-1, windows, 3, lag_count).sum(axis=1)  26.3 us
    reshape x2, local copies, waits for them, and re-layouts, shards(): jnp.transpose(pieces, (1, 2, 3, 0, 4))  26.1 us
  transfers between devices with their start and end apart: 2, of which 2 were waited for; matrix products, arithmetic and copies ran while one was open for 0% of the time, Pallas kernels for 0%

commit v1 on v0

--- a/solution.py
+++ b/solution.py
@@ -15,9 +15,14 @@
 phase_floor = 0.1
 
 
+def cut_the_knots(state, axis_key):
+    x_next = jnp.sum(jax.lax.all_gather(state, axis_key), axis=0)
+    return x_next
+
+
 def broadcast(block, axis, source):
     block = jnp.where(lax.axis_index(axis) == source, block, jnp.zeros_like(block))
-    return lax.psum(block, axis)
+    return cut_the_knots(block, axis)
 
 
 def band_matrix():

time: 766 us -> 757 us (0.988)
  waiting for transfers between devices: 103 us -> 20.2 us
  blocking collectives: 224 us -> 297 us
    all_gather x0 -> x4, blocking collectives: none -> 93.6 us  [cut_the_knots(): x_next = jnp.sum(jax.lax.all_gather(state, axis_key), axis=0)]
    psum x1 -> x0, waiting for transfers between devices: 82.3 us -> none  [broadcast(): return lax.psum(block, axis)]
    all_to_all x1, blocking collectives: 213 us -> 193 us  [shards(): lax.all_to_all(buffer, 'chan', split_axis=1, concat_axis=1, tiled=True)]
    unnamed x3 -> x2, waiting for transfers between devices: 20.2 us -> 20.2 us
    unnamed x10 -> x8, local copies, waits for them, and re-layouts: 42.2 us -> 42.2 us
  transfers between devices with their start and end apart: 2 -> 1, of which waited for: 2 -> 1; matrix products, arithmetic and copies ran while one was open for 0% -> 0% of each run, Pallas kernels for 0% -> 0%
where the time goes in v1:
time: 757 us; the launch traced here: 749 us
  blocking collectives  297 us (39%)
  local copies, waits for them, and re-layouts  191 us (25%)
  other arithmetic  141 us (19%)
  matrix products  63.9 us (8%)
  between operations  23.8 us (3%)
  waiting for transfers between devices  20.2 us (3%)
  loops' own time  11.3 us (1%)
    all_to_all x1, blocking collectives, shards(): lax.all_to_all(buffer, 'chan', split_axis=1, concat_axis=1, tiled=True)  193 us
    all_gather x4, blocking collectives, cut_the_knots(): x_next = jnp.sum(jax.lax.all_gather(state, axis_key), axis=0)  93.6 us
    another operation x17, other arithmetic  78.3 us
    dot_general x16, matrix products, correlate_block(): jnp.dot(cross_rows, lag_table(first_lag, lag_count), preferred_element_ty...  59.6 us
    unnamed x8, local copies, waits for them, and re-layouts  42.2 us
    gather x3, local copies, waits for them, and re-layouts, gather_rows(): block_rows[chosen]  31.8 us
    reduce_sum x16, other arithmetic, correlate_block(): return terms.reshape(-1, windows, 3, lag_count).sum(axis=1)  26.3 us
    reshape x2, local copies, waits for them, and re-layouts, shards(): jnp.transpose(pieces, (1, 2, 3, 0, 4))  26.1 us
  transfers between devices with their start and end apart: 1, of which 1 were waited for; matrix products, arithmetic and copies ran while one was open for 0% of the time, Pallas kernels for 0%

profile of v1, /device:TPU:0, one launch (start us, length us, event | category | flops | bytes accessed | tf_op | source)
XLA Modules:
  0.0 748.6 jit_solution(2772717627859626809)
XLA Ops:
  29.4 25.3 %all_gather.16 = bf16[16,4,2,1024]{3,1,2,0:T(4,128)(2,1)S(1)} all-gather(bf16[1,4,2,1024]{3,1,2,0:T(4,128)(2,1)S(1)} %copy.75), channel_id=1, replica_groups=mesh['chan'=16,'win'=8] {'chan'}, dimensions={0}, use_global_device_ids=true | all-gather | bytes 278528 | tf_op jit(solution)/shard_map/all_gather | solution.py:19
  54.8 23.2 %all_gather.17 = bf16[16,4,2,1024]{3,1,2,0:T(4,128)(2,1)S(1)} all-gather(bf16[1,4,2,1024]{3,1,2,0:T(4,128)(2,1)S(1)} %copy.76), channel_id=1, replica_groups=mesh['chan'=16,'win'=8] {'chan'}, dimensions={0}, use_global_device_ids=true | all-gather | bytes 278528 | tf_op jit(solution)/shard_map/all_gather | solution.py:19
  78.2 21.6 %all_gather.18 = bf16[16,4,2,1024]{3,1,2,0:T(4,128)(2,1)S(1)} all-gather(bf16[1,4,2,1024]{3,1,2,0:T(4,128)(2,1)S(1)} %copy.77), channel_id=1, replica_groups=mesh['chan'=16,'win'=8] {'chan'}, dimensions={0}, use_global_device_ids=true | all-gather | bytes 278528 | tf_op jit(solution)/shard_map/all_gather | solution.py:19
  99.9 23.6 %all_gather.19 = bf16[16,4,2,1024]{3,1,2,0:T(4,128)(2,1)S(1)} all-gather(bf16[1,4,2,1024]{3,1,2,0:T(4,128)(2,1)S(1)} %copy.78), channel_id=1, replica_groups=mesh['chan'=16,'win'=8] {'chan'}, dimensions={0}, use_global_device_ids=true | all-gather | bytes 278528 | tf_op jit(solution)/shard_map/all_gather | solution.py:19
  133.6 226.1 %while.12 = (s32[]{:T(128)}, f32[16,192,3,256]{3,1,2,0:T(8,128)}, s32[16]{0:T(128)S(1)}, bf16[768,2048]{1,0:T(8,128)(2,1)}, s32[]{:T(128)}, /*index=5*/s32[1]{0:T(128)}) while((s32[]{:T(128)}, f32[16,192,3,256]{3,1,2,0:T(8,128)}, s32[16]{0:T(128)S(1)}, bf16[768,2048]{1,0:T(8,128)(2,1)}, s32[]{:T(128)}, /*index=5*/s32[1]{0:T(128)}) %tuple.55), condition=%wide.region_6.7_spmd, body=%wide.region_4.6_spmd.sunk | while | flops 1626916352 | bytes 25373280 | solution.py:127
  134.8 4.7 fusion.55
  148.9 4.7 fusion.55
  163.0 4.7 fusion.55
  177.2 4.7 fusion.55
  191.3 4.7 fusion.55
  205.4 4.7 fusion.55
  219.5 4.7 fusion.55
  233.6 4.7 fusion.55
  247.7 4.7 fusion.55
  261.9 4.7 fusion.55
  276.0 4.7 fusion.55
  290.1 4.7 fusion.55
  304.2 4.7 fusion.55
  332.4 4.7 fusion.55
  346.6 4.7 fusion.55
  359.7 13.8 %copy.118 = f32[16,4,48,3,256]{4,0,2,3,1:T(8,128)} copy(f32[16,4,48,3,256]{4,2,1,3,0:T(8,128)} %bitcast.102) | data formatting | bytes 18874368 | tf_op jit(solution)/shard_map/reshape | solution.py:128
  373.5 11.3 %reshape.178 = f32[4,48,3,4096]{3,1,2,0:T(8,128)} reshape(f32[4,48,3,16,256]{4,3,1,2,0:T(8,128)} %bitcast.100) | data formatting | bytes 18874368 | tf_op jit(solution)/shard_map/reshape | solution.py:129
  384.9 14.8 %copy.82 = f32[4,48,3,4096]{3,2,1,0:T(4,128)} copy(f32[4,48,3,4096]{3,1,2,0:T(8,128)} %reshape.178) | data formatting | bytes 18874368 | tf_op jit(solution)/shard_map/reshape | solution.py:129
  400.1 31.5 %gather_fusion = f32[384,3,4096]{2,1,0:T(4,128)} fusion(f32[4,48,3,4096]{3,2,1,0:T(4,128)} %copy.82, s32[384]{0:T(512)S(1)} %reshape.184), kind=kCustom, calls=%fused_computation | custom fusion | bytes 37751808 | tf_op jit(solution)/shard_map/vmap()/gather | solution.py:87
  431.7 12.7 %copy_multiply_fusion = f32[4,16,6,3,4096]{4,2,1,0,3:T(8,128)S(1)} fusion(f32[4,16,6,3,4096]{4,3,2,1,0:T(4,128)} %bitcast.99, f32[4,16,6]{2,1,0:T(8,128)S(1)} %reshape.183), kind=kLoop, calls=%fused_computation.30 | loop fusion | flops 4718592 | bytes 37750272 | tf_op jit(solution)/shard_map/mul | solution.py:88
  444.4 17.2 %copy.85 = f32[4,16,6,3,4096]{4,0,3,2,1:T(4,128)} copy(f32[4,16,6,3,4096]{4,2,1,0,3:T(8,128)S(1)} %copy_multiply_fusion) | data formatting | bytes 37748736 | tf_op jit(solution)/shard_map/mul | solution.py:88
  461.6 192.7 %all_to_all.10 = f32[4,16,6,3,4096]{4,0,3,2,1:T(4,128)} all-to-all(f32[4,16,6,3,4096]{4,0,3,2,1:T(4,128)} %copy.85), channel_id=1, replica_groups=mesh['chan'=16,'win'=8] {'chan'}, dimensions={1} | all-to-all | bytes 37748736 | tf_op jit(solution)/shard_map/all_to_all | solution.py:133
  654.3 10.5 %reduce_sum.96 = f32[4,6,3,4096]{3,0,2,1:T(4,128)S(1)} reduce(f32[4,16,6,3,4096]{4,0,3,2,1:T(4,128)} %all_to_all.10, f32[]{:T(128)} %constant.119.clone.1), dimensions={1}, to_apply=%region_7.8 | reduce | flops 4423680 | bytes 20054020 | tf_op jit(solution)/shard_map/reduce_sum | solution.py:99
  665.1 16.9 %copy.91 = f32[4,2,3,4096]{1,0,2,3:T(4,128)} copy(f32[4,2,3,4096]{3,0,2,1:T(4,128)S(1)} %reduce_sum.98) | data formatting | bytes 786432
  682.0 18.1 %reshape.197 = f32[4096,24]{1,0:T(8,128)} reshape(f32[4096,3,4,2]{3,2,1,0:T(4,128)} %bitcast.98) | data formatting | bytes 786432
  700.2 11.1 %all_to_all.11 = f32[4,16,6]{2,0,1:T(4,128)S(1)} all-to-all(f32[4,16,6]{2,0,1:T(4,128)S(1)} %copy.89), channel_id=1, replica_groups=mesh['chan'=16,'win'=8] {'chan'}, dimensions={1} | all-to-all | bytes 3072 | tf_op jit(solution)/shard_map/all_to_all | solution.py:134
  711.5 20.2 %reduce-scatter.4.cloned.1.call-done = f32[512,24]{1,0:T(8,128)} async-done(((f32[4096,24]{1,0:T(8,128)}), f32[512,24]{1,0:T(8,128)}) %reduce-scatter.4.cloned.1.call-update) | async-done | bytes 49168
  (254 shorter events, 178.2 us)
Async XLA Ops:
  6.5 725.2 %reduce-scatter.4.cloned.1.call-start = ((), (), s32[]{:S(2)}) async-start(), calls=%async_computation.3 | async-start | bytes 2359296
  128.3 1.9 copy-start
Sparse Core Ops, SparseCore 0:
  700.3 31.3 reduce-scatter.3
